TPU v7x, 256 devices: a whole 4x4x8 slice. The times are simulated.
256 devices in a mesh: row: 16 (over x_lo, y, core), col: 16 (over z, x_hi).
Axes of the slice: x: 4 (x_hi: 2, x_lo: 2; x = x_hi * 2 + x_lo), y: 4, z: 8, core: 2. Of those that a mesh axis runs over, the one named last changes fastest.
Arguments:
- green: bfloat16 [32768, 32768], P('row', 'col'), may hold values from -0.046875 to 0.046875
- mask: int32 [128, 128], P('row', 'col'), may hold values from 0 to 1, as said below
- probes: bfloat16 [32768, 256], P('col', 'row'), may hold values from -6 to 6
Outputs:
- sketch: float32 [32768, 256], P('row', 'col')
- adjoint: float32 [32768, 256], P('col', 'row')
Inputs may be any that keep to these rules, and one draw needn't show every extreme that they name: `mask`: block row i belongs to gauge i % 6 and time block i // 6; block column j to window j // 8. A block is 1 when its time block is no earlier than the window's onset plus a travel delay of its gauge and subfault block.
All inputs are finite; a program needn't handle non-finite values.
Results may differ from a plain program's by a relative error of at most 0.0022.
Values may be sent and summed in bfloat16 or wider, within the bound.
A program may use at most 128 MiB of HBM per device.

v0:
```python
import jax
import jax.numpy as jnp
from jax import lax
from jax.sharding import PartitionSpec as P


def local(green, mask, probes):
    row_blocks, col_blocks = mask.shape
    block_size = green.shape[0] // row_blocks
    shaped = green.reshape(row_blocks, block_size, col_blocks, block_size)
    tiles = (shaped * mask.astype(jnp.bfloat16)[:, None, :, None]).reshape(green.shape)
    all_probes = lax.all_gather(probes, "row", axis=1, tiled=True)
    partial_sketch = jnp.dot(tiles, all_probes, preferred_element_type=jnp.float32)
    own_sketch = lax.psum_scatter(partial_sketch, "col", scatter_dimension=1, tiled=True)
    lowered = lax.all_gather(own_sketch.astype(jnp.bfloat16), "col", axis=1, tiled=True)
    term_t = lax.dot_general(
        lowered, tiles, (((0,), (0,)), ((), ())), preferred_element_type=jnp.float32
    )
    adjoint_t = lax.psum_scatter(term_t, "row", scatter_dimension=0, tiled=True)
    return (own_sketch, adjoint_t.T)


def solution(mesh):
    in_specs = (P("row", "col"), P("row", "col"), P("col", "row"))
    out_specs = (P("row", "col"), P("col", "row"))
    return jax.shard_map(local, mesh=mesh, in_specs=in_specs, out_specs=out_specs, check_vma=False)
```

profile of v0, /device:TPU:32, one launch (start us, length us, event | category | flops | bytes accessed | tf_op | source)
XLA Modules:
  0.0 419.4 jit_solution(13793577123540415991)
XLA Ops:
  7.2 0.0 all-gather.3.cloned.1.call-start
  7.2 0.7 all-gather.3.cloned.1.call-update
  7.9 0.0 reduce-scatter.3.cloned.1.call-start
  7.9 0.7 convert_element_type.6
  8.6 3.8 mul.11
  12.5 10.3 %copy.5 = bf16[256,8,8,256]{3,1,2,0:T(8,128)(2,1)} copy(bf16[256,8,8,256]{3,2,1,0:T(8,128)(2,1)} %bitcast.9) | data formatting | bytes 16777216
  22.8 10.5 %mul.13 = bf16[2048,2048]{1,0:T(8,128)(2,1)} multiply(bf16[2048,2048]{1,0:T(8,128)(2,1)} %param.3, bf16[2048,2048]{1,0:T(8,128)(2,1)} %bitcast.8) | non-fusion elementwise | flops 4194304 | bytes 25165824 | tf_op jit(solution)/shard_map/mul | solution.py:11
  33.3 14.2 %all-gather.3.cloned.1.call-done = bf16[2048,256]{0,1:T(8,128)(2,1)} async-done(((bf16[2048,16]{0,1:T(8,128)(2,1)}), bf16[2048,256]{0,1:T(8,128)(2,1)}) %all-gather.3.cloned.1.call-update) | async-done | bytes 1048592 | tf_op jit(solution)/shard_map/all_gather | solution.py:12
  47.5 7.3 %fusion = f32[2048,256]{0,1:T(8,128)} fusion(bf16[2048,2048]{1,0:T(8,128)(2,1)} %mul.13, bf16[2048,256]{0,1:T(8,128)(2,1)} %all-gather.3.cloned.1.call-done), kind=kOutput, calls=%fused_computation | convolution fusion | flops 2147483648 | bytes 11534336 | tf_op jit(solution)/shard_map/dot_general | solution.py:13
  54.8 0.0 reduce-scatter.3.cloned.1.call-update
  54.8 0.0 all-gather.5.cloned.1.call-start
  54.9 207.1 %reduce-scatter.3.cloned.1.call-done = f32[2048,16]{0,1:T(8,128)} async-done(((f32[2048,256]{0,1:T(8,128)}), f32[2048,16]{0,1:T(8,128)}) %reduce-scatter.3.cloned.1.call-update) | async-done | bytes 131088 | tf_op jit(solution)/shard_map/reduce_scatter | solution.py:14
  262.0 1.5 convert_element_type.7
  263.5 0.0 all-gather.5.cloned.1.call-update
  263.5 0.0 reduce-scatter.5.cloned.1.call-start
  263.6 78.4 %all-gather.5.cloned.1.call-done = bf16[2048,256]{0,1:T(8,128)(2,1)} async-done(((bf16[2048,16]{0,1:T(8,128)(2,1)}), bf16[2048,256]{0,1:T(8,128)(2,1)}) %all-gather.5.cloned.1.call-update) | async-done | bytes 1048592 | tf_op jit(solution)/shard_map/all_gather | solution.py:15
  341.9 7.4 %fusion.1 = f32[256,2048]{1,0:T(8,128)} fusion(bf16[2048,256]{0,1:T(8,128)(2,1)} %all-gather.5.cloned.1.call-done, bf16[2048,2048]{1,0:T(8,128)(2,1)} %mul.13), kind=kOutput, calls=%fused_computation.1 | convolution fusion | flops 2147483648 | bytes 11534336 | tf_op jit(solution)/shard_map/dot_general | solution.py:16
  349.3 0.0 reduce-scatter.5.cloned.1.call-update
  349.4 63.5 %reduce-scatter.5.cloned.1.call-done = f32[16,2048]{1,0:T(8,128)} async-done(((f32[256,2048]{1,0:T(8,128)}), f32[16,2048]{1,0:T(8,128)}) %reduce-scatter.5.cloned.1.call-update) | async-done | bytes 131088 | tf_op jit(solution)/shard_map/reduce_scatter | solution.py:19
Async XLA Ops:
  7.2 40.3 %all-gather.3.cloned.1.call-start = ((), (), s32[]{:S(2)}) async-start(), calls=%async_computation.2 | async-start | bytes 1114112 | tf_op jit(solution)/shard_map/all_gather | solution.py:12
  7.9 254.1 %reduce-scatter.3.cloned.1.call-start = ((), (), s32[]{:S(2)}) async-start(), calls=%async_computation.3 | async-start | bytes 2228224 | tf_op jit(solution)/shard_map/reduce_scatter | solution.py:14
  54.8 287.1 %all-gather.5.cloned.1.call-start = ((), (), s32[]{:S(2)}) async-start(), calls=%async_computation.4 | async-start | bytes 1114112 | tf_op jit(solution)/shard_map/all_gather | solution.py:15
  263.5 149.3 %reduce-scatter.5.cloned.1.call-start = ((), (), s32[]{:S(2)}) async-start(), calls=%async_computation.5 | async-start | bytes 2228224 | tf_op jit(solution)/shard_map/reduce_scatter | solution.py:19
Sparse Core Ops, SparseCore 0:
  9.8 37.5 all-gather.2
  55.0 206.9 reduce-scatter.2
  265.1 76.7 all-gather.4
  349.5 63.3 reduce-scatter.4
where the time goes:
time: 420 us; the launch traced here: 419 us
  waiting for transfers between devices  364 us (87%)
  matrix products  14.7 us (4%)
  local copies, waits for them, and re-layouts  14.1 us (3%)
  between operations  13.8 us (3%)
  other arithmetic  12.8 us (3%)
    reduce_scatter x1, waiting for transfers between devices, local(): lax.psum_scatter(partial_sketch, 'col', scatter_dimension=1, tiled=True)  207 us
    all_gather x1, waiting for transfers between devices, local(): lax.all_gather(own_sketch.astype(jnp.bfloat16), 'col', axis=1, tiled=True)  78.4 us
    reduce_scatter x1, waiting for transfers between devices, local(): adjoint_t = lax.psum_scatter(term_t, 'row', scatter_dimension=0, tiled=True)  63.5 us
    all_gather x1, waiting for transfers between devices, local(): all_probes = lax.all_gather(probes, 'row', axis=1, tiled=True)  14.2 us
    mul x1, other arithmetic, local(): shaped * mask.astype(jnp.bfloat16)[:, None, :, None]  10.5 us
    unnamed x1, local copies, waits for them, and re-layouts  10.3 us
  transfers between devices with their start and end apart: 4, of which 4 were waited for; matrix products, arithmetic and copies ran while one was open for 6% of the time, Pallas kernels for 0%

commit v1 on v0

--- a/solution.py
+++ b/solution.py
@@ -12,7 +12,11 @@
     all_probes = lax.all_gather(probes, "row", axis=1, tiled=True)
     partial_sketch = jnp.dot(tiles, all_probes, preferred_element_type=jnp.float32)
     own_sketch = lax.psum_scatter(partial_sketch, "col", scatter_dimension=1, tiled=True)
-    lowered = lax.all_gather(own_sketch.astype(jnp.bfloat16), "col", axis=1, tiled=True)
+    own = own_sketch.astype(jnp.bfloat16)
+    size = lax.axis_size("col")
+    blocks = jnp.stack([own for _ in range(size)])
+    blocks = lax.all_to_all(blocks, "col", split_axis=0, concat_axis=0)
+    lowered = jnp.concatenate(blocks, axis=1)
     term_t = lax.dot_general(
         lowered, tiles, (((0,), (0,)), ((), ())), preferred_element_type=jnp.float32
     )

time: 420 us -> 369 us (0.88)
  waiting for transfers between devices: 364 us -> 284 us
  blocking collectives: 0 us -> 30.3 us
    all_gather x1 -> x0, waiting for transfers between devices: 78.4 us -> none  [local(): lax.all_gather(own_sketch.astype(jnp.bfloat16), 'col', axis=1, tiled=True)]
    all_to_all x0 -> x1, blocking collectives: none -> 30.3 us  [local(): blocks = lax.all_to_all(blocks, 'col', split_axis=0, concat_axis=0)]
  transfers between devices with their start and end apart: 4 -> 3, of which waited for: 4 -> 3; matrix products, arithmetic and copies ran while one was open for 6% -> 7% of each run, Pallas kernels for 0% -> 0%
where the time goes in v1:
time: 369 us
  waiting for transfers between devices  284 us (77%)
  blocking collectives  30.3 us (8%)
  matrix products  14.4 us (4%)
  local copies, waits for them, and re-layouts  14.2 us (4%)
  between operations  13.8 us (4%)
  other arithmetic  12.1 us (3%)
    reduce_scatter x1, waiting for transfers between devices, local(): lax.psum_scatter(partial_sketch, 'col', scatter_dimension=1, tiled=True)  207 us
    reduce_scatter x1, waiting for transfers between devices, local(): adjoint_t = lax.psum_scatter(term_t, 'row', scatter_dimension=0, tiled=True)  62.4 us
    all_to_all x1, blocking collectives, local(): blocks = lax.all_to_all(blocks, 'col', split_axis=0, concat_axis=0)  30.3 us
    all_gather x1, waiting for transfers between devices, local(): all_probes = lax.all_gather(probes, 'row', axis=1, tiled=True)  14.2 us
    mul x1, other arithmetic, local(): shaped * mask.astype(jnp.bfloat16)[:, None, :, None]  10.5 us
    unnamed x1, local copies, waits for them, and re-layouts  10.3 us
  transfers between devices with their start and end apart: 3, of which 3 were waited for; matrix products, arithmetic and copies ran while one was open for 7% of the time, Pallas kernels for 0%

profile of v1, /device:TPU:32, one launch (start us, length us, event | category | flops | bytes accessed | tf_op | source)
XLA Modules:
  0.0 369.2 jit_solution(15955650981381141620)
XLA Ops:
  7.2 0.0 all-gather.2.cloned.1.call-start
  7.2 0.7 all-gather.2.cloned.1.call-update
  7.9 0.0 reduce-scatter.3.cloned.1.call-start
  7.9 0.7 convert_element_type.6
  8.6 3.8 %mul.11 = bf16[8,256,8,256]{3,2,1,0:T(8,128)(2,1)} broadcast(bf16[8,8]{1,0:T(8,128)(2,1)S(1)} %convert_element_type.6), dimensions={0,2} | broadcast | bytes 8388736 | tf_op jit(solution)/shard_map/mul | solution.py:11
  12.5 10.3 %copy.6 = bf16[256,8,8,256]{3,1,2,0:T(8,128)(2,1)} copy(bf16[256,8,8,256]{3,2,1,0:T(8,128)(2,1)} %bitcast.12) | data formatting | bytes 16777216
  22.7 10.5 %mul.13 = bf16[2048,2048]{1,0:T(8,128)(2,1)} multiply(bf16[2048,2048]{1,0:T(8,128)(2,1)} %param.3, bf16[2048,2048]{1,0:T(8,128)(2,1)} %bitcast.11) | non-fusion elementwise | flops 4194304 | bytes 25165824 | tf_op jit(solution)/shard_map/mul | solution.py:11
  33.3 14.2 %all-gather.2.cloned.1.call-done = bf16[2048,256]{0,1:T(8,128)(2,1)} async-done(((bf16[2048,16]{0,1:T(8,128)(2,1)}), bf16[2048,256]{0,1:T(8,128)(2,1)}) %all-gather.2.cloned.1.call-update) | async-done | bytes 1048592 | tf_op jit(solution)/shard_map/all_gather | solution.py:12
  47.5 7.3 %fusion = f32[2048,256]{0,1:T(8,128)} fusion(bf16[2048,2048]{1,0:T(8,128)(2,1)} %mul.13, bf16[2048,256]{0,1:T(8,128)(2,1)} %all-gather.2.cloned.1.call-done), kind=kOutput, calls=%fused_computation | convolution fusion | flops 2147483648 | bytes 11534336 | tf_op jit(solution)/shard_map/dot_general | solution.py:13
  54.8 0.0 reduce-scatter.3.cloned.1.call-update
  54.8 0.0 reduce-scatter.5.cloned.1.call-start
  54.9 206.9 %reduce-scatter.3.cloned.1.call-done = f32[2048,16]{0,1:T(8,128)} async-done(((f32[2048,256]{0,1:T(8,128)}), f32[2048,16]{0,1:T(8,128)}) %reduce-scatter.3.cloned.1.call-update) | async-done | bytes 131088 | tf_op jit(solution)/shard_map/reduce_scatter | solution.py:14
  261.8 0.9 convert_element_type.7
  262.7 0.1 stack.2
  262.9 30.3 %all_to_all.5 = bf16[16,2048,16]{1,2,0:T(8,128)(2,1)S(1)} all-to-all(bf16[16,2048,16]{1,2,0:T(8,128)(2,1)S(1)} %stack.2), channel_id=1, replica_groups=mesh['row'=16,'col'=16] {'col'}, dimensions={0} | all-to-all | bytes 2097152 | tf_op jit(solution)/shard_map/all_to_all | solution.py:18
  293.2 7.1 %fusion.1 = f32[256,2048]{1,0:T(8,128)} fusion(bf16[2048,256]{0,1:T(8,128)(2,1)S(1)} %bitcast.13, bf16[2048,2048]{1,0:T(8,128)(2,1)} %mul.13), kind=kOutput, calls=%fused_computation.1 | convolution fusion | flops 2147483648 | bytes 11534336 | tf_op jit(solution)/shard_map/dot_general | solution.py:20
  300.2 0.0 reduce-scatter.5.cloned.1.call-update
  300.3 62.4 %reduce-scatter.5.cloned.1.call-done = f32[16,2048]{1,0:T(8,128)} async-done(((f32[256,2048]{1,0:T(8,128)}), f32[16,2048]{1,0:T(8,128)}) %reduce-scatter.5.cloned.1.call-update) | async-done | bytes 131088 | tf_op jit(solution)/shard_map/reduce_scatter | solution.py:23
Async XLA Ops:
  7.2 40.3 %all-gather.2.cloned.1.call-start = ((), (), s32[]{:S(2)}) async-start(), calls=%async_computation.3 | async-start | bytes 1114112 | tf_op jit(solution)/shard_map/all_gather | solution.py:12
  7.9 253.9 %reduce-scatter.3.cloned.1.call-start = ((), (), s32[]{:S(2)}) async-start(), calls=%async_computation.4 | async-start | bytes 2228224 | tf_op jit(solution)/shard_map/reduce_scatter | solution.py:14
  54.8 307.8 %reduce-scatter.5.cloned.1.call-start = ((), (), s32[]{:S(2)}) async-start(), calls=%async_computation.5 | async-start | bytes 2228224 | tf_op jit(solution)/shard_map/reduce_scatter | solution.py:23
Sparse Core Ops, SparseCore 0:
  9.8 37.5 all-gather.1
  55.0 206.8 reduce-scatter.2
  300.4 62.2 reduce-scatter.4
